TPU v7x, 512 devices: a whole 4x4x16 slice. The times are simulated.
512 devices in a mesh: gz: 16 (over y, x), pa: 32 (over z, core).
Axes of the slice: x: 4, y: 4, z: 16, core: 2. Of those that a mesh axis runs over, the one named last changes fastest.
Arguments:
- particles: float32 [6, 1048576], P(None, ('gz', 'pa')), may hold values from -6 to 6
- slice_index: int32 [1048576], P(('gz', 'pa')), may hold values from 0 to 127
- moving: int32 [16, 32, 2], P('gz', 'pa'), may hold values from 0 to 384, as said below
- decay_rate: float32 [8], replicated, may hold values from 0.3 to 600
- wake_freq: float32 [8], replicated, may hold values from -3.140625 to 3.140625
- wake_amp: float32 [4, 8], replicated, may hold values from -3 to 3
Outputs:
- wake_kick: float32 [3, 2048], P(None, 'gz')
- particles_out: float32 [6, 1441792], P(None, ('gz', 'pa'))
Inputs may be any that keep to these rules, and one draw needn't show every extreme that they name: `moving`: each entry is at most 384, and some entry equals 384.
All inputs are finite; a program needn't handle non-finite values.
Results may differ from a plain program's by a relative error of at most 0.0003.
Values sent between devices are 32-bit elements; how exact they have to be, the bound alone decides.
No kernel may reach another device: no remote copies, remote signals or barrier semaphores. Data moves between devices by JAX's collectives and lax.ppermute only.
A program may use at most 64 MiB of HBM per device.

v0:
```python
import math
import jax
import jax.numpy as jnp
from jax import lax
from jax.sharding import PartitionSpec as P

S_DEV = 128
two_pi = 6.283185307179586
adjust_horiz = 0.269
adjust_vert = 0.355
chroma_horiz = 0.05
chroma_vert = 0.04
curve_horiz = 0.02
curve_vert = -0.015
detune_self = 0.03
detune_cross = -0.02
voltage = 0.05
synch_phase = 0.3
slippage = 0.1


def from_behind_2(value, axis, steps):
    count = lax.axis_size(axis)
    leading, last = (max(0, -steps), min(count, count - steps))
    return lax.ppermute(value, axis, [(source, source + steps) for source in range(leading, last)])


def complex_mul(first, second):
    return jnp.stack(
        [first[0] * second[0] - first[1] * second[1], first[0] * second[1] + first[1] * second[0]]
    )


def powers(damping, wake_freq, distance):
    envelope = jnp.exp(-damping[:, None] * distance[None, :])
    angles = wake_freq[:, None] * distance[None, :]
    return (envelope * jnp.cos(angles), envelope * jnp.sin(angles))


def toeplitz(wave):
    slab_width = wave.shape[0]
    row_index = lax.broadcasted_iota(jnp.int32, (slab_width, slab_width), 0)
    col_index = lax.broadcasted_iota(jnp.int32, (slab_width, slab_width), 1)
    offset = col_index - row_index
    picked = jnp.take(wave, jnp.clip(offset, 0, slab_width - 1))
    return jnp.where(offset > 0, picked, jnp.float32(0.0))


def slab_tables(decay_rate, wake_freq, wake_amp, slab_width, slice_total):
    damping = decay_rate / slice_total
    norm_trans = jnp.sqrt(2.0 * damping)
    norm_long = jnp.sqrt(damping * damping + wake_freq * wake_freq)
    coef_real = jnp.stack(
        [wake_amp[0] * norm_trans, wake_amp[0] * norm_trans, wake_amp[2] * norm_long], axis=1
    )
    coef_imag = jnp.stack(
        [wake_amp[1] * norm_trans, wake_amp[1] * norm_trans, wake_amp[3] * norm_long], axis=1
    )
    distance = jnp.arange(slab_width, dtype=jnp.float32)
    near_re, near_im = powers(damping, wake_freq, distance)
    far_re, far_im = powers(damping, wake_freq, slab_width - distance)
    whole_re, whole_im = powers(damping, wake_freq, jnp.full((1,), slab_width, jnp.float32))
    factor = jnp.stack(
        [jnp.broadcast_to(whole_re, coef_real.shape), jnp.broadcast_to(whole_im, coef_real.shape)]
    )
    wave_trans = jnp.sum(
        norm_trans[:, None] * (wake_amp[0][:, None] * near_re - wake_amp[1][:, None] * near_im),
        axis=0,
    )
    wave_long = jnp.sum(
        norm_long[:, None] * (wake_amp[2][:, None] * near_re - wake_amp[3][:, None] * near_im),
        axis=0,
    )
    return (
        toeplitz(wave_trans),
        toeplitz(wave_long),
        near_re,
        near_im,
        far_re,
        far_im,
        factor,
        coef_real,
        coef_imag,
    )


def slab_summary(moments, tables):
    highest = lax.Precision.HIGHEST
    return jnp.stack(
        [
            jnp.dot(tables[4], moments.T, precision=highest),
            jnp.dot(tables[5], moments.T, precision=highest),
        ]
    )


def slab_kick(moments, carried, tables):
    highest = lax.Precision.HIGHEST
    trans_kick = jnp.dot(moments[0:2], tables[0], precision=highest)
    long_kick = jnp.dot(moments[2:3], tables[1], precision=highest)
    coef_re = tables[7] * carried[0] - tables[8] * carried[1]
    coef_im = tables[7] * carried[1] + tables[8] * carried[0]
    incoming = jnp.dot(coef_re.T, tables[2], precision=highest) - jnp.dot(
        coef_im.T, tables[3], precision=highest
    )
    return jnp.concatenate([trans_kick, long_kick], axis=0) + incoming


def moment_values(particles, mean_fill):
    root_fill = math.sqrt(mean_fill)
    return jnp.stack(
        [
            particles[0] / root_fill,
            particles[2] / root_fill,
            jnp.full_like(particles[0], 1.0 / mean_fill),
        ]
    )


def deposit(values, index, segments):
    return jax.vmap(lambda column: jax.ops.segment_sum(column, index, num_segments=segments))(
        values
    )


def one_turn(coords, kicks):
    hor_pos = coords[0]
    hor_mom = coords[1] + kicks[0]
    ver_pos = coords[2]
    ver_mom = coords[3] + kicks[1]
    lag_pos = coords[4]
    energy_dev = coords[5] + kicks[2]
    action_x = 0.5 * (hor_pos * hor_pos + hor_mom * hor_mom)
    action_y = 0.5 * (ver_pos * ver_pos + ver_mom * ver_mom)
    phase_x = two_pi * (
        adjust_horiz
        + chroma_horiz * energy_dev
        + curve_horiz * energy_dev * energy_dev
        + detune_self * action_x
        + detune_cross * action_y
    )
    phase_y = two_pi * (
        adjust_vert
        + chroma_vert * energy_dev
        + curve_vert * energy_dev * energy_dev
        + detune_self * action_y
        + detune_cross * action_x
    )
    cosine_x = jnp.cos(phase_x)
    sine_x = jnp.sin(phase_x)
    cosine_y = jnp.cos(phase_y)
    sine_y = jnp.sin(phase_y)
    new_energy = energy_dev - voltage * (jnp.sin(synch_phase + lag_pos) - math.sin(synch_phase))
    new_lag = lag_pos - slippage * new_energy
    return jnp.stack(
        [
            cosine_x * hor_pos + sine_x * hor_mom,
            cosine_x * hor_mom - sine_x * hor_pos,
            cosine_y * ver_pos + sine_y * ver_mom,
            cosine_y * ver_mom - sine_y * ver_pos,
            new_lag,
            new_energy,
        ]
    )


def upstream(own_summary, factor, slab_count):

    def advance(step_index, carried):
        return from_behind_2(complex_mul(factor, carried) + own_summary, "gz", 1)

    return lax.fori_loop(0, slab_count - 1, advance, jnp.zeros_like(own_summary))


def body(particles, slice_index, moving, decay_rate, wake_freq, wake_amp):
    slab_count = lax.axis_size("gz")
    member_count = lax.axis_size("pa")
    local_count = particles.shape[1]
    slab_width = S_DEV
    tables = slab_tables(decay_rate, wake_freq, wake_amp, slab_width, slab_width * slab_count)
    mean_fill = local_count * member_count / slab_width
    values = moment_values(particles, mean_fill)
    partial_moments = deposit(values, slice_index, slab_width)
    moments = lax.psum(partial_moments, "pa")
    carried = upstream(slab_summary(moments, tables), tables[6], slab_count)
    wake_kick = slab_kick(moments, carried, tables)
    per_particle = jnp.take(wake_kick, slice_index, axis=1)
    capacity = local_count * 3 // 16
    head_count = moving[0, 0, 0]
    tail_count = moving[0, 0, 1]
    slot_index = lax.broadcasted_iota(jnp.int32, (1, capacity), 1)
    leaving_head = slot_index < head_count
    leaving_tail = slot_index >= capacity - tail_count
    zero_value = jnp.float32(0.0)
    tail_start = local_count - capacity
    moved_all = one_turn(particles, per_particle)
    head_part = moved_all[:, :capacity]
    tail_part = moved_all[:, tail_start:]
    head_send = jnp.where(leaving_head, head_part, zero_value)
    tail_send = jnp.where(leaving_tail, tail_part, zero_value)
    from_behind = from_behind_2(head_send, "gz", -1)
    from_ahead = from_behind_2(tail_send, "gz", 1)
    head_kept = jnp.where(leaving_head, zero_value, head_part)
    tail_kept = jnp.where(leaving_tail, zero_value, tail_part)
    middle_part = moved_all[:, capacity:tail_start]
    particles_out = jnp.concatenate(
        [from_behind, head_kept, middle_part, tail_kept, from_ahead], axis=1
    )
    return (wake_kick, particles_out)


def solution(mesh):
    return jax.shard_map(
        body,
        mesh=mesh,
        in_specs=(P(None, ("gz", "pa")), P(("gz", "pa")), P("gz", "pa", None), P(), P(), P()),
        out_specs=(P(None, "gz"), P(None, ("gz", "pa"))),
        check_vma=False,
    )
```

profile of v0, /device:TPU:16, one launch (start us, length us, event | category | flops | bytes accessed | tf_op | source)
XLA Modules:
  0.0 447.7 jit_solution(7515340950392063301)
XLA Ops:
  0.6 0.9 broadcast_multiply_fusion.1
  2.4 11.5 %scatter_custom_fusion = f32[3,128]{0,1:T(8,128)S(1)} fusion(s32[2048]{0:T(1024)S(1)} %copy-done.1, f32[2048,3]{1,0:T(8,128)S(1)} %copy.80, f32[]{:T(128)} %constant.22.clone.1), kind=kCustom, calls=%fused_computation.37 | custom fusion | flops 6144 | bytes 1540 | tf_op jit(solution)/shard_map/vmap()/scatter-add | solution.py:121
  14.0 99.1 %psum.7 = f32[3,128]{0,1:T(8,128)S(1)} all-reduce(f32[3,128]{0,1:T(8,128)S(1)} %scatter_custom_fusion), channel_id=1, replica_groups=mesh['gz'=16,'pa'=32] {'pa'}, use_global_device_ids=true, to_apply=%region_1.0 | all-reduce | flops 384 | bytes 3072 | tf_op jit(solution)/shard_map/psum | solution.py:184
  113.9 114.3 %while.11 = (s32[]{:T(128)}, f32[2,8,3]{1,0,2:T(2,128)S(1)}, f32[2,8,3]{1,0,2:T(2,128)S(1)}, f32[8]{0:T(128)S(1)}, f32[8]{0:T(128)S(1)}, /*index=5*/s32[]{:T(128)}) while((s32[]{:T(128)}, f32[2,8,3]{1,0,2:T(2,128)S(1)}, f32[2,8,3]{1,0,2:T(2,128)S(1)}, f32[8]{0:T(128)S(1)}, f32[8]{0:T(128)S(1)}, /*index=5*/s32[]{:T(128)}) %tuple.64), condition=%wide.region_5.7_spmd.clone, body=%wide.region_4.6_spmd.clone.sunk | while | flops 242 | bytes 1901 | solution.py:172
  113.9 3.4 collective-permute-start
  117.4 4.2 collective-permute-done
  121.6 1.9 collective-permute-start
  123.5 5.7 %collective-permute-done = f32[2,8,3]{1,0,2:T(2,128)S(1)} collective-permute-done((f32[2,8,3]{1,0,2:T(2,128)S(1)}, f32[2,8,3]{1,0,2:T(2,128)S(1)}, u32[]{:S(2)}, u32[]{:S(2)}) %collective-permute-start) | collective-permute-done | bytes 224 | tf_op jit(solution)/shard_map/while/body/eval_jaxpr/ppermute | solution.py:25
  129.2 1.9 collective-permute-start
  131.1 5.7 %collective-permute-done = f32[2,8,3]{1,0,2:T(2,128)S(1)} collective-permute-done((f32[2,8,3]{1,0,2:T(2,128)S(1)}, f32[2,8,3]{1,0,2:T(2,128)S(1)}, u32[]{:S(2)}, u32[]{:S(2)}) %collective-permute-start) | collective-permute-done | bytes 224 | tf_op jit(solution)/shard_map/while/body/eval_jaxpr/ppermute | solution.py:25
  136.8 1.9 collective-permute-start
  138.7 5.7 %collective-permute-done = f32[2,8,3]{1,0,2:T(2,128)S(1)} collective-permute-done((f32[2,8,3]{1,0,2:T(2,128)S(1)}, f32[2,8,3]{1,0,2:T(2,128)S(1)}, u32[]{:S(2)}, u32[]{:S(2)}) %collective-permute-start) | collective-permute-done | bytes 224 | tf_op jit(solution)/shard_map/while/body/eval_jaxpr/ppermute | solution.py:25
  144.4 1.9 collective-permute-start
  146.4 5.7 %collective-permute-done = f32[2,8,3]{1,0,2:T(2,128)S(1)} collective-permute-done((f32[2,8,3]{1,0,2:T(2,128)S(1)}, f32[2,8,3]{1,0,2:T(2,128)S(1)}, u32[]{:S(2)}, u32[]{:S(2)}) %collective-permute-start) | collective-permute-done | bytes 224 | tf_op jit(solution)/shard_map/while/body/eval_jaxpr/ppermute | solution.py:25
  152.0 1.9 collective-permute-start
  154.0 5.7 %collective-permute-done = f32[2,8,3]{1,0,2:T(2,128)S(1)} collective-permute-done((f32[2,8,3]{1,0,2:T(2,128)S(1)}, f32[2,8,3]{1,0,2:T(2,128)S(1)}, u32[]{:S(2)}, u32[]{:S(2)}) %collective-permute-start) | collective-permute-done | bytes 224 | tf_op jit(solution)/shard_map/while/body/eval_jaxpr/ppermute | solution.py:25
  159.7 1.9 collective-permute-start
  161.6 5.7 %collective-permute-done = f32[2,8,3]{1,0,2:T(2,128)S(1)} collective-permute-done((f32[2,8,3]{1,0,2:T(2,128)S(1)}, f32[2,8,3]{1,0,2:T(2,128)S(1)}, u32[]{:S(2)}, u32[]{:S(2)}) %collective-permute-start) | collective-permute-done | bytes 224 | tf_op jit(solution)/shard_map/while/body/eval_jaxpr/ppermute | solution.py:25
  167.3 1.9 collective-permute-start
  169.2 5.7 %collective-permute-done = f32[2,8,3]{1,0,2:T(2,128)S(1)} collective-permute-done((f32[2,8,3]{1,0,2:T(2,128)S(1)}, f32[2,8,3]{1,0,2:T(2,128)S(1)}, u32[]{:S(2)}, u32[]{:S(2)}) %collective-permute-start) | collective-permute-done | bytes 224 | tf_op jit(solution)/shard_map/while/body/eval_jaxpr/ppermute | solution.py:25
  174.9 1.9 collective-permute-start
  176.8 5.7 %collective-permute-done = f32[2,8,3]{1,0,2:T(2,128)S(1)} collective-permute-done((f32[2,8,3]{1,0,2:T(2,128)S(1)}, f32[2,8,3]{1,0,2:T(2,128)S(1)}, u32[]{:S(2)}, u32[]{:S(2)}) %collective-permute-start) | collective-permute-done | bytes 224 | tf_op jit(solution)/shard_map/while/body/eval_jaxpr/ppermute | solution.py:25
  182.5 1.9 collective-permute-start
  184.5 5.7 %collective-permute-done = f32[2,8,3]{1,0,2:T(2,128)S(1)} collective-permute-done((f32[2,8,3]{1,0,2:T(2,128)S(1)}, f32[2,8,3]{1,0,2:T(2,128)S(1)}, u32[]{:S(2)}, u32[]{:S(2)}) %collective-permute-start) | collective-permute-done | bytes 224 | tf_op jit(solution)/shard_map/while/body/eval_jaxpr/ppermute | solution.py:25
  190.2 1.9 collective-permute-start
  192.1 5.7 %collective-permute-done = f32[2,8,3]{1,0,2:T(2,128)S(1)} collective-permute-done((f32[2,8,3]{1,0,2:T(2,128)S(1)}, f32[2,8,3]{1,0,2:T(2,128)S(1)}, u32[]{:S(2)}, u32[]{:S(2)}) %collective-permute-start) | collective-permute-done | bytes 224 | tf_op jit(solution)/shard_map/while/body/eval_jaxpr/ppermute | solution.py:25
  197.8 1.9 collective-permute-start
  199.7 5.7 %collective-permute-done = f32[2,8,3]{1,0,2:T(2,128)S(1)} collective-permute-done((f32[2,8,3]{1,0,2:T(2,128)S(1)}, f32[2,8,3]{1,0,2:T(2,128)S(1)}, u32[]{:S(2)}, u32[]{:S(2)}) %collective-permute-start) | collective-permute-done | bytes 224 | tf_op jit(solution)/shard_map/while/body/eval_jaxpr/ppermute | solution.py:25
  205.4 1.9 collective-permute-start
  207.3 5.7 %collective-permute-done = f32[2,8,3]{1,0,2:T(2,128)S(1)} collective-permute-done((f32[2,8,3]{1,0,2:T(2,128)S(1)}, f32[2,8,3]{1,0,2:T(2,128)S(1)}, u32[]{:S(2)}, u32[]{:S(2)}) %collective-permute-start) | collective-permute-done | bytes 224 | tf_op jit(solution)/shard_map/while/body/eval_jaxpr/ppermute | solution.py:25
  213.0 1.9 collective-permute-start
  214.9 5.7 %collective-permute-done = f32[2,8,3]{1,0,2:T(2,128)S(1)} collective-permute-done((f32[2,8,3]{1,0,2:T(2,128)S(1)}, f32[2,8,3]{1,0,2:T(2,128)S(1)}, u32[]{:S(2)}, u32[]{:S(2)}) %collective-permute-start) | collective-permute-done | bytes 224 | tf_op jit(solution)/shard_map/while/body/eval_jaxpr/ppermute | solution.py:25
  220.6 1.9 collective-permute-start
  222.6 5.7 %collective-permute-done = f32[2,8,3]{1,0,2:T(2,128)S(1)} collective-permute-done((f32[2,8,3]{1,0,2:T(2,128)S(1)}, f32[2,8,3]{1,0,2:T(2,128)S(1)}, u32[]{:S(2)}, u32[]{:S(2)}) %collective-permute-start) | collective-permute-done | bytes 224 | tf_op jit(solution)/shard_map/while/body/eval_jaxpr/ppermute | solution.py:25
  228.4 97.2 %gather_fusion.1 = f32[16384]{0:T(1024)S(1)} fusion(f32[128]{0:T(128)S(1)} %get-tuple-element.75, s32[16384]{0:T(1024)S(1)} %bitcast_clamp_fusion), kind=kCustom, calls=%fused_computation.clone | custom fusion | bytes 196608 | tf_op jit(solution)/shard_map/jit(_take)/gather | solution.py:45
  325.8 97.2 %gather_fusion.2 = f32[16384]{0:T(1024)S(1)} fusion(f32[128]{0:T(128)S(1)} %get-tuple-element.76, s32[16384]{0:T(1024)S(1)} %bitcast_clamp_fusion), kind=kCustom, calls=%fused_computation.1.clone | custom fusion | bytes 196608 | tf_op jit(solution)/shard_map/jit(_take)/gather | solution.py:45
  423.8 0.5 copy-done.3
  424.3 5.5 %gather_fusion = f32[2048,3]{1,0:T(8,128)S(1)} fusion(f32[3,128]{0,1:T(8,128)S(1)} %copy.82, s32[2048]{0:T(1024)S(1)} %fusion.32), kind=kCustom, calls=%fused_computation.2 | custom fusion | bytes 57344 | tf_op jit(solution)/shard_map/jit(_take)/gather | solution.py:187
  430.1 0.8 copy-done
  431.0 0.5 multiply_subtract_fusion.1
  431.6 0.6 fusion.68
  432.2 0.7 iota_compare_fusion.1
  432.9 0.5 multiply_subtract_fusion.3
  433.7 1.9 collective-permute-start.1
  436.3 3.0 collective-permute-done.1
  439.4 1.9 collective-permute-start.2
  441.3 5.8 %collective-permute-done.2 = f32[6,384]{1,0:T(8,128)S(1)} collective-permute-done((f32[6,384]{1,0:T(8,128)S(1)}, f32[6,384]{1,0:T(8,128)S(1)}, u32[]{:S(2)}, u32[]{:S(2)}) %collective-permute-start.2) | collective-permute-done | bytes 9248 | tf_op jit(solution)/shard_map/ppermute | solution.py:25
  447.1 0.6 copy-done.5
  (77 shorter events, 4.0 us)
Async XLA Ops:
  1.7 0.7 copy-start.1
  13.9 99.1 %copy-start.2 = (f32[4,8]{1,0:T(4,128)S(1)}, f32[4,8]{1,0:T(4,128)}, u32[]{:S(2)}) copy-start(f32[4,8]{1,0:T(4,128)} %param.15) | copy-start | bytes 388
  13.9 99.1 %copy-start.6 = (f32[8]{0:T(128)S(1)}, f32[8]{0:T(128)}, u32[]{:S(2)}) copy-start(f32[8]{0:T(128)} %param.13) | copy-start | bytes 100
  13.9 99.1 %copy-start.7 = (f32[8]{0:T(128)S(1)}, f32[8]{0:T(128)}, u32[]{:S(2)}) copy-start(f32[8]{0:T(128)} %param.14) | copy-start | bytes 100
  113.9 7.6 %collective-permute-start = (f32[2,8,3]{1,0,2:T(2,128)S(1)}, f32[2,8,3]{1,0,2:T(2,128)S(1)}, u32[]{:S(2)}, u32[]{:S(2)}) collective-permute-start(f32[2,8,3]{1,0,2:T(2,128)S(1)} %maximum_add_fusion.2), channel_id=1, source_target_pairs={{0,32},{32,64},{64,96},{96,128},{128,160},{160,192},{192,224},{224... | collective-permute-start | bytes 584 | tf_op jit(solution)/shard_map/while/body/eval_jaxpr/ppermute | solution.py:25
  121.6 7.6 %collective-permute-start = (f32[2,8,3]{1,0,2:T(2,128)S(1)}, f32[2,8,3]{1,0,2:T(2,128)S(1)}, u32[]{:S(2)}, u32[]{:S(2)}) collective-permute-start(f32[2,8,3]{1,0,2:T(2,128)S(1)} %maximum_add_fusion.2), channel_id=1, source_target_pairs={{0,32},{32,64},{64,96},{96,128},{128,160},{160,192},{192,224},{224... | collective-permute-start | bytes 584 | tf_op jit(solution)/shard_map/while/body/eval_jaxpr/ppermute | solution.py:25
  129.2 7.6 %collective-permute-start = (f32[2,8,3]{1,0,2:T(2,128)S(1)}, f32[2,8,3]{1,0,2:T(2,128)S(1)}, u32[]{:S(2)}, u32[]{:S(2)}) collective-permute-start(f32[2,8,3]{1,0,2:T(2,128)S(1)} %maximum_add_fusion.2), channel_id=1, source_target_pairs={{0,32},{32,64},{64,96},{96,128},{128,160},{160,192},{192,224},{224... | collective-permute-start | bytes 584 | tf_op jit(solution)/shard_map/while/body/eval_jaxpr/ppermute | solution.py:25
  136.8 7.6 %collective-permute-start = (f32[2,8,3]{1,0,2:T(2,128)S(1)}, f32[2,8,3]{1,0,2:T(2,128)S(1)}, u32[]{:S(2)}, u32[]{:S(2)}) collective-permute-start(f32[2,8,3]{1,0,2:T(2,128)S(1)} %maximum_add_fusion.2), channel_id=1, source_target_pairs={{0,32},{32,64},{64,96},{96,128},{128,160},{160,192},{192,224},{224... | collective-permute-start | bytes 584 | tf_op jit(solution)/shard_map/while/body/eval_jaxpr/ppermute | solution.py:25
  144.4 7.6 %collective-permute-start = (f32[2,8,3]{1,0,2:T(2,128)S(1)}, f32[2,8,3]{1,0,2:T(2,128)S(1)}, u32[]{:S(2)}, u32[]{:S(2)}) collective-permute-start(f32[2,8,3]{1,0,2:T(2,128)S(1)} %maximum_add_fusion.2), channel_id=1, source_target_pairs={{0,32},{32,64},{64,96},{96,128},{128,160},{160,192},{192,224},{224... | collective-permute-start | bytes 584 | tf_op jit(solution)/shard_map/while/body/eval_jaxpr/ppermute | solution.py:25
  152.0 7.6 %collective-permute-start = (f32[2,8,3]{1,0,2:T(2,128)S(1)}, f32[2,8,3]{1,0,2:T(2,128)S(1)}, u32[]{:S(2)}, u32[]{:S(2)}) collective-permute-start(f32[2,8,3]{1,0,2:T(2,128)S(1)} %maximum_add_fusion.2), channel_id=1, source_target_pairs={{0,32},{32,64},{64,96},{96,128},{128,160},{160,192},{192,224},{224... | collective-permute-start | bytes 584 | tf_op jit(solution)/shard_map/while/body/eval_jaxpr/ppermute | solution.py:25
  159.7 7.6 %collective-permute-start = (f32[2,8,3]{1,0,2:T(2,128)S(1)}, f32[2,8,3]{1,0,2:T(2,128)S(1)}, u32[]{:S(2)}, u32[]{:S(2)}) collective-permute-start(f32[2,8,3]{1,0,2:T(2,128)S(1)} %maximum_add_fusion.2), channel_id=1, source_target_pairs={{0,32},{32,64},{64,96},{96,128},{128,160},{160,192},{192,224},{224... | collective-permute-start | bytes 584 | tf_op jit(solution)/shard_map/while/body/eval_jaxpr/ppermute | solution.py:25
  167.3 7.6 %collective-permute-start = (f32[2,8,3]{1,0,2:T(2,128)S(1)}, f32[2,8,3]{1,0,2:T(2,128)S(1)}, u32[]{:S(2)}, u32[]{:S(2)}) collective-permute-start(f32[2,8,3]{1,0,2:T(2,128)S(1)} %maximum_add_fusion.2), channel_id=1, source_target_pairs={{0,32},{32,64},{64,96},{96,128},{128,160},{160,192},{192,224},{224... | collective-permute-start | bytes 584 | tf_op jit(solution)/shard_map/while/body/eval_jaxpr/ppermute | solution.py:25
  174.9 7.6 %collective-permute-start = (f32[2,8,3]{1,0,2:T(2,128)S(1)}, f32[2,8,3]{1,0,2:T(2,128)S(1)}, u32[]{:S(2)}, u32[]{:S(2)}) collective-permute-start(f32[2,8,3]{1,0,2:T(2,128)S(1)} %maximum_add_fusion.2), channel_id=1, source_target_pairs={{0,32},{32,64},{64,96},{96,128},{128,160},{160,192},{192,224},{224... | collective-permute-start | bytes 584 | tf_op jit(solution)/shard_map/while/body/eval_jaxpr/ppermute | solution.py:25
  182.5 7.6 %collective-permute-start = (f32[2,8,3]{1,0,2:T(2,128)S(1)}, f32[2,8,3]{1,0,2:T(2,128)S(1)}, u32[]{:S(2)}, u32[]{:S(2)}) collective-permute-start(f32[2,8,3]{1,0,2:T(2,128)S(1)} %maximum_add_fusion.2), channel_id=1, source_target_pairs={{0,32},{32,64},{64,96},{96,128},{128,160},{160,192},{192,224},{224... | collective-permute-start | bytes 584 | tf_op jit(solution)/shard_map/while/body/eval_jaxpr/ppermute | solution.py:25
  190.2 7.6 %collective-permute-start = (f32[2,8,3]{1,0,2:T(2,128)S(1)}, f32[2,8,3]{1,0,2:T(2,128)S(1)}, u32[]{:S(2)}, u32[]{:S(2)}) collective-permute-start(f32[2,8,3]{1,0,2:T(2,128)S(1)} %maximum_add_fusion.2), channel_id=1, source_target_pairs={{0,32},{32,64},{64,96},{96,128},{128,160},{160,192},{192,224},{224... | collective-permute-start | bytes 584 | tf_op jit(solution)/shard_map/while/body/eval_jaxpr/ppermute | solution.py:25
  197.8 7.6 %collective-permute-start = (f32[2,8,3]{1,0,2:T(2,128)S(1)}, f32[2,8,3]{1,0,2:T(2,128)S(1)}, u32[]{:S(2)}, u32[]{:S(2)}) collective-permute-start(f32[2,8,3]{1,0,2:T(2,128)S(1)} %maximum_add_fusion.2), channel_id=1, source_target_pairs={{0,32},{32,64},{64,96},{96,128},{128,160},{160,192},{192,224},{224... | collective-permute-start | bytes 584 | tf_op jit(solution)/shard_map/while/body/eval_jaxpr/ppermute | solution.py:25
  205.4 7.6 %collective-permute-start = (f32[2,8,3]{1,0,2:T(2,128)S(1)}, f32[2,8,3]{1,0,2:T(2,128)S(1)}, u32[]{:S(2)}, u32[]{:S(2)}) collective-permute-start(f32[2,8,3]{1,0,2:T(2,128)S(1)} %maximum_add_fusion.2), channel_id=1, source_target_pairs={{0,32},{32,64},{64,96},{96,128},{128,160},{160,192},{192,224},{224... | collective-permute-start | bytes 584 | tf_op jit(solution)/shard_map/while/body/eval_jaxpr/ppermute | solution.py:25
  213.0 7.6 %collective-permute-start = (f32[2,8,3]{1,0,2:T(2,128)S(1)}, f32[2,8,3]{1,0,2:T(2,128)S(1)}, u32[]{:S(2)}, u32[]{:S(2)}) collective-permute-start(f32[2,8,3]{1,0,2:T(2,128)S(1)} %maximum_add_fusion.2), channel_id=1, source_target_pairs={{0,32},{32,64},{64,96},{96,128},{128,160},{160,192},{192,224},{224... | collective-permute-start | bytes 584 | tf_op jit(solution)/shard_map/while/body/eval_jaxpr/ppermute | solution.py:25
  220.6 7.6 %collective-permute-start = (f32[2,8,3]{1,0,2:T(2,128)S(1)}, f32[2,8,3]{1,0,2:T(2,128)S(1)}, u32[]{:S(2)}, u32[]{:S(2)}) collective-permute-start(f32[2,8,3]{1,0,2:T(2,128)S(1)} %maximum_add_fusion.2), channel_id=1, source_target_pairs={{0,32},{32,64},{64,96},{96,128},{128,160},{160,192},{192,224},{224... | collective-permute-start | bytes 584 | tf_op jit(solution)/shard_map/while/body/eval_jaxpr/ppermute | solution.py:25
  423.7 0.6 copy-start.3
  430.1 0.9 copy-start
  431.0 0.7 copy-start.4
  433.7 5.6 %collective-permute-start.1 = (f32[6,384]{1,0:T(8,128)S(1)}, f32[6,384]{1,0:T(8,128)S(1)}, u32[]{:S(2)}, u32[]{:S(2)}) collective-permute-start(f32[6,384]{1,0:T(8,128)S(1)} %slice_select_fusion.1), channel_id=1, source_target_pairs={{32,0},{64,32},{96,64},{128,96},{160,128},{192,160},{224,192},{256... | collective-permute-start | bytes 27656 | tf_op jit(solution)/shard_map/ppermute | solution.py:25
  439.4 7.7 %collective-permute-start.2 = (f32[6,384]{1,0:T(8,128)S(1)}, f32[6,384]{1,0:T(8,128)S(1)}, u32[]{:S(2)}, u32[]{:S(2)}) collective-permute-start(f32[6,384]{1,0:T(8,128)S(1)} %get-tuple-element.109), channel_id=1, source_target_pairs={{0,32},{32,64},{64,96},{96,128},{128,160},{160,192},{192,224},{224... | collective-permute-start | bytes 27656 | tf_op jit(solution)/shard_map/ppermute | solution.py:25
  447.1 0.6 copy-start.5
where the time goes:
time: 450 us; the launch traced here: 448 us
  local copies, waits for them, and re-layouts  204 us (45%)
  blocking collectives  99.1 us (22%)
  waiting for transfers between devices  92.3 us (21%)
  starting transfers between devices  34.1 us (8%)
  other arithmetic  15 us (3%)
    gather x2, local copies, waits for them, and re-layouts, toeplitz(): picked = jnp.take(wave, jnp.clip(offset, 0, slab_width - 1))  194 us
    psum x1, blocking collectives, body(): moments = lax.psum(partial_moments, 'pa')  99.1 us
    ppermute x17, waiting for transfers between devices, from_behind_2(): lax.ppermute(value, axis, [(source, source + steps) for source in range(l...  92.3 us
    ppermute x17, starting transfers between devices, from_behind_2(): lax.ppermute(value, axis, [(source, source + steps) for source in range(l...  34.1 us
    scatter-add x1, other arithmetic, deposit(): jax.ops.segment_sum(column, index, num_segments=segments)  11.5 us
  transfers between devices with their start and end apart: 17, of which 17 were waited for; matrix products, arithmetic and copies ran while one was open for 0% of the time, Pallas kernels for 0%

commit v1 on v0

--- a/solution.py
+++ b/solution.py
@@ -181,7 +181,10 @@
     mean_fill = local_count * member_count / slab_width
     values = moment_values(particles, mean_fill)
     partial_moments = deposit(values, slice_index, slab_width)
-    moments = lax.psum(partial_moments, "pa")
+    _run_zone = lambda packet, shard_axis: jax.lax.all_gather(packet, axis_name=shard_axis).sum(
+        axis=0
+    )
+    moments = _run_zone(partial_moments, "pa")
     carried = upstream(slab_summary(moments, tables), tables[6], slab_count)
     wake_kick = slab_kick(moments, carried, tables)
     per_particle = jnp.take(wake_kick, slice_index, axis=1)

time: 450 us -> 388 us (0.86)
  blocking collectives: 99.1 us -> 36.4 us
    psum x1 -> x0, blocking collectives: 99.1 us -> none  [body(): moments = lax.psum(partial_moments, 'pa')]
    all_gather x0 -> x1, blocking collectives: none -> 36.4 us  [body(): jax.lax.all_gather(packet, axis_name=shard_axis).sum(axis=0)]
where the time goes in v1:
time: 388 us; the launch traced here: 385 us
  local copies, waits for them, and re-layouts  205 us (53%)
  waiting for transfers between devices  92.3 us (24%)
  blocking collectives  36.4 us (9%)
  starting transfers between devices  34.1 us (9%)
  other arithmetic  15.1 us (4%)
    gather x2, local copies, waits for them, and re-layouts, toeplitz(): picked = jnp.take(wave, jnp.clip(offset, 0, slab_width - 1))  194 us
    ppermute x17, waiting for transfers between devices, from_behind_2(): lax.ppermute(value, axis, [(source, source + steps) for source in range(l...  92.3 us
    all_gather x1, blocking collectives, body(): jax.lax.all_gather(packet, axis_name=shard_axis).sum(axis=0)  36.4 us
    ppermute x17, starting transfers between devices, from_behind_2(): lax.ppermute(value, axis, [(source, source + steps) for source in range(l...  34.1 us
    scatter-add x1, other arithmetic, deposit(): jax.ops.segment_sum(column, index, num_segments=segments)  11.5 us
  transfers between devices with their start and end apart: 17, of which 17 were waited for; matrix products, arithmetic and copies ran while one was open for 0% of the time, Pallas kernels for 0%

profile of v1, /device:TPU:16, one launch (start us, length us, event | category | flops | bytes accessed | tf_op | source)
XLA Modules:
  0.0 385.5 jit_solution(815268996868322272)
XLA Ops:
  0.6 0.9 broadcast_multiply_fusion.1
  2.4 11.5 %scatter_custom_fusion = f32[3,128]{0,1:T(8,128)S(1)} fusion(s32[2048]{0:T(1024)S(1)} %copy-done.1, f32[2048,3]{1,0:T(8,128)S(1)} %copy.109, f32[]{:T(128)} %constant.22.clone.1), kind=kCustom, calls=%fused_computation.35 | custom fusion | flops 6144 | bytes 1540 | tf_op jit(solution)/shard_map/vmap()/scatter-add | solution.py:121
  14.0 36.4 %all-gather.1 = f32[32,3,128]{2,1,0:T(4,128)S(1)} all-gather(f32[1,3,128]{2,1,0:T(4,128)S(1)} %copy.110), channel_id=2, replica_groups=mesh['gz'=16,'pa'=32] {'pa'}, dimensions={0}, use_global_device_ids=true | all-gather | bytes 50688 | tf_op jit(solution)/shard_map/all_gather | solution.py:184
  50.4 0.6 copy-done.2
  51.7 114.3 %while.11 = (s32[]{:T(128)}, f32[2,8,3]{1,0,2:T(2,128)S(1)}, f32[2,8,3]{1,0,2:T(2,128)S(1)}, f32[8]{0:T(128)S(1)}, f32[8]{0:T(128)S(1)}, /*index=5*/s32[]{:T(128)}) while((s32[]{:T(128)}, f32[2,8,3]{1,0,2:T(2,128)S(1)}, f32[2,8,3]{1,0,2:T(2,128)S(1)}, f32[8]{0:T(128)S(1)}, f32[8]{0:T(128)S(1)}, /*index=5*/s32[]{:T(128)}) %tuple.65), condition=%wide.region_5.7_spmd.clone, body=%wide.region_4.6_spmd.clone.sunk | while | flops 242 | bytes 1901 | solution.py:172
  51.8 3.4 collective-permute-start
  55.2 4.2 %collective-permute-done = f32[2,8,3]{1,0,2:T(2,128)S(1)} collective-permute-done((f32[2,8,3]{1,0,2:T(2,128)S(1)}, f32[2,8,3]{1,0,2:T(2,128)S(1)}, u32[]{:S(2)}, u32[]{:S(2)}) %collective-permute-start) | collective-permute-done | bytes 224 | tf_op jit(solution)/shard_map/while/body/eval_jaxpr/ppermute | solution.py:25
  59.4 1.9 collective-permute-start
  61.3 5.7 %collective-permute-done = f32[2,8,3]{1,0,2:T(2,128)S(1)} collective-permute-done((f32[2,8,3]{1,0,2:T(2,128)S(1)}, f32[2,8,3]{1,0,2:T(2,128)S(1)}, u32[]{:S(2)}, u32[]{:S(2)}) %collective-permute-start) | collective-permute-done | bytes 224 | tf_op jit(solution)/shard_map/while/body/eval_jaxpr/ppermute | solution.py:25
  67.0 1.9 collective-permute-start
  69.0 5.7 %collective-permute-done = f32[2,8,3]{1,0,2:T(2,128)S(1)} collective-permute-done((f32[2,8,3]{1,0,2:T(2,128)S(1)}, f32[2,8,3]{1,0,2:T(2,128)S(1)}, u32[]{:S(2)}, u32[]{:S(2)}) %collective-permute-start) | collective-permute-done | bytes 224 | tf_op jit(solution)/shard_map/while/body/eval_jaxpr/ppermute | solution.py:25
  74.7 1.9 collective-permute-start
  76.6 5.7 %collective-permute-done = f32[2,8,3]{1,0,2:T(2,128)S(1)} collective-permute-done((f32[2,8,3]{1,0,2:T(2,128)S(1)}, f32[2,8,3]{1,0,2:T(2,128)S(1)}, u32[]{:S(2)}, u32[]{:S(2)}) %collective-permute-start) | collective-permute-done | bytes 224 | tf_op jit(solution)/shard_map/while/body/eval_jaxpr/ppermute | solution.py:25
  82.3 1.9 collective-permute-start
  84.2 5.7 %collective-permute-done = f32[2,8,3]{1,0,2:T(2,128)S(1)} collective-permute-done((f32[2,8,3]{1,0,2:T(2,128)S(1)}, f32[2,8,3]{1,0,2:T(2,128)S(1)}, u32[]{:S(2)}, u32[]{:S(2)}) %collective-permute-start) | collective-permute-done | bytes 224 | tf_op jit(solution)/shard_map/while/body/eval_jaxpr/ppermute | solution.py:25
  89.9 1.9 collective-permute-start
  91.8 5.7 %collective-permute-done = f32[2,8,3]{1,0,2:T(2,128)S(1)} collective-permute-done((f32[2,8,3]{1,0,2:T(2,128)S(1)}, f32[2,8,3]{1,0,2:T(2,128)S(1)}, u32[]{:S(2)}, u32[]{:S(2)}) %collective-permute-start) | collective-permute-done | bytes 224 | tf_op jit(solution)/shard_map/while/body/eval_jaxpr/ppermute | solution.py:25
  97.5 1.9 collective-permute-start
  99.4 5.7 %collective-permute-done = f32[2,8,3]{1,0,2:T(2,128)S(1)} collective-permute-done((f32[2,8,3]{1,0,2:T(2,128)S(1)}, f32[2,8,3]{1,0,2:T(2,128)S(1)}, u32[]{:S(2)}, u32[]{:S(2)}) %collective-permute-start) | collective-permute-done | bytes 224 | tf_op jit(solution)/shard_map/while/body/eval_jaxpr/ppermute | solution.py:25
  105.1 1.9 collective-permute-start
  107.1 5.7 %collective-permute-done = f32[2,8,3]{1,0,2:T(2,128)S(1)} collective-permute-done((f32[2,8,3]{1,0,2:T(2,128)S(1)}, f32[2,8,3]{1,0,2:T(2,128)S(1)}, u32[]{:S(2)}, u32[]{:S(2)}) %collective-permute-start) | collective-permute-done | bytes 224 | tf_op jit(solution)/shard_map/while/body/eval_jaxpr/ppermute | solution.py:25
  112.8 1.9 collective-permute-start
  114.7 5.7 %collective-permute-done = f32[2,8,3]{1,0,2:T(2,128)S(1)} collective-permute-done((f32[2,8,3]{1,0,2:T(2,128)S(1)}, f32[2,8,3]{1,0,2:T(2,128)S(1)}, u32[]{:S(2)}, u32[]{:S(2)}) %collective-permute-start) | collective-permute-done | bytes 224 | tf_op jit(solution)/shard_map/while/body/eval_jaxpr/ppermute | solution.py:25
  120.4 1.9 collective-permute-start
  122.3 5.7 %collective-permute-done = f32[2,8,3]{1,0,2:T(2,128)S(1)} collective-permute-done((f32[2,8,3]{1,0,2:T(2,128)S(1)}, f32[2,8,3]{1,0,2:T(2,128)S(1)}, u32[]{:S(2)}, u32[]{:S(2)}) %collective-permute-start) | collective-permute-done | bytes 224 | tf_op jit(solution)/shard_map/while/body/eval_jaxpr/ppermute | solution.py:25
  128.0 1.9 collective-permute-start
  129.9 5.7 %collective-permute-done = f32[2,8,3]{1,0,2:T(2,128)S(1)} collective-permute-done((f32[2,8,3]{1,0,2:T(2,128)S(1)}, f32[2,8,3]{1,0,2:T(2,128)S(1)}, u32[]{:S(2)}, u32[]{:S(2)}) %collective-permute-start) | collective-permute-done | bytes 224 | tf_op jit(solution)/shard_map/while/body/eval_jaxpr/ppermute | solution.py:25
  135.6 1.9 collective-permute-start
  137.5 5.7 %collective-permute-done = f32[2,8,3]{1,0,2:T(2,128)S(1)} collective-permute-done((f32[2,8,3]{1,0,2:T(2,128)S(1)}, f32[2,8,3]{1,0,2:T(2,128)S(1)}, u32[]{:S(2)}, u32[]{:S(2)}) %collective-permute-start) | collective-permute-done | bytes 224 | tf_op jit(solution)/shard_map/while/body/eval_jaxpr/ppermute | solution.py:25
  143.2 1.9 collective-permute-start
  145.2 5.7 %collective-permute-done = f32[2,8,3]{1,0,2:T(2,128)S(1)} collective-permute-done((f32[2,8,3]{1,0,2:T(2,128)S(1)}, f32[2,8,3]{1,0,2:T(2,128)S(1)}, u32[]{:S(2)}, u32[]{:S(2)}) %collective-permute-start) | collective-permute-done | bytes 224 | tf_op jit(solution)/shard_map/while/body/eval_jaxpr/ppermute | solution.py:25
  150.9 1.9 collective-permute-start
  152.8 5.7 %collective-permute-done = f32[2,8,3]{1,0,2:T(2,128)S(1)} collective-permute-done((f32[2,8,3]{1,0,2:T(2,128)S(1)}, f32[2,8,3]{1,0,2:T(2,128)S(1)}, u32[]{:S(2)}, u32[]{:S(2)}) %collective-permute-start) | collective-permute-done | bytes 224 | tf_op jit(solution)/shard_map/while/body/eval_jaxpr/ppermute | solution.py:25
  158.5 1.9 collective-permute-start
  160.4 5.7 %collective-permute-done = f32[2,8,3]{1,0,2:T(2,128)S(1)} collective-permute-done((f32[2,8,3]{1,0,2:T(2,128)S(1)}, f32[2,8,3]{1,0,2:T(2,128)S(1)}, u32[]{:S(2)}, u32[]{:S(2)}) %collective-permute-start) | collective-permute-done | bytes 224 | tf_op jit(solution)/shard_map/while/body/eval_jaxpr/ppermute | solution.py:25
  166.2 97.2 %gather_fusion.2 = f32[16384]{0:T(1024)S(1)} fusion(f32[128]{0:T(128)S(1)} %get-tuple-element.81, s32[16384]{0:T(1024)S(1)} %bitcast_clamp_fusion), kind=kCustom, calls=%fused_computation.1.clone | custom fusion | bytes 196608 | tf_op jit(solution)/shard_map/jit(_take)/gather | solution.py:45
  263.4 97.2 %gather_fusion.1 = f32[16384]{0:T(1024)S(1)} fusion(f32[128]{0:T(128)S(1)} %get-tuple-element.80, s32[16384]{0:T(1024)S(1)} %bitcast_clamp_fusion), kind=kCustom, calls=%fused_computation.clone | custom fusion | bytes 196608 | tf_op jit(solution)/shard_map/jit(_take)/gather | solution.py:45
  362.1 5.5 %gather_fusion = f32[2048,3]{1,0:T(8,128)S(1)} fusion(f32[3,128]{0,1:T(8,128)S(1)} %copy.113, s32[2048]{0:T(1024)S(1)} %fusion.31), kind=kCustom, calls=%fused_computation.2 | custom fusion | bytes 57344 | tf_op jit(solution)/shard_map/jit(_take)/gather | solution.py:190
  367.9 0.8 copy-done
  368.8 0.5 multiply_subtract_fusion.1
  369.4 0.6 fusion.67
  370.0 0.7 iota_compare_fusion.1
  370.7 0.5 multiply_subtract_fusion.3
  371.5 1.9 collective-permute-start.1
  374.1 3.0 collective-permute-done.1
  377.1 1.9 collective-permute-start.2
  379.1 5.8 %collective-permute-done.2 = f32[6,384]{1,0:T(8,128)S(1)} collective-permute-done((f32[6,384]{1,0:T(8,128)S(1)}, f32[6,384]{1,0:T(8,128)S(1)}, u32[]{:S(2)}, u32[]{:S(2)}) %collective-permute-start.2) | collective-permute-done | bytes 9248 | tf_op jit(solution)/shard_map/ppermute | solution.py:25
  384.8 0.6 copy-done.5
  (79 shorter events, 4.3 us)
Async XLA Ops:
  1.7 0.7 copy-start.1
  50.4 0.7 copy-start.2
  50.4 0.7 copy-start.6
  50.4 0.7 copy-start.7
  51.8 7.6 %collective-permute-start = (f32[2,8,3]{1,0,2:T(2,128)S(1)}, f32[2,8,3]{1,0,2:T(2,128)S(1)}, u32[]{:S(2)}, u32[]{:S(2)}) collective-permute-start(f32[2,8,3]{1,0,2:T(2,128)S(1)} %maximum_add_fusion.2), channel_id=1, source_target_pairs={{0,32},{32,64},{64,96},{96,128},{128,160},{160,192},{192,224},{224... | collective-permute-start | bytes 584 | tf_op jit(solution)/shard_map/while/body/eval_jaxpr/ppermute | solution.py:25
  59.4 7.6 %collective-permute-start = (f32[2,8,3]{1,0,2:T(2,128)S(1)}, f32[2,8,3]{1,0,2:T(2,128)S(1)}, u32[]{:S(2)}, u32[]{:S(2)}) collective-permute-start(f32[2,8,3]{1,0,2:T(2,128)S(1)} %maximum_add_fusion.2), channel_id=1, source_target_pairs={{0,32},{32,64},{64,96},{96,128},{128,160},{160,192},{192,224},{224... | collective-permute-start | bytes 584 | tf_op jit(solution)/shard_map/while/body/eval_jaxpr/ppermute | solution.py:25
  67.0 7.6 %collective-permute-start = (f32[2,8,3]{1,0,2:T(2,128)S(1)}, f32[2,8,3]{1,0,2:T(2,128)S(1)}, u32[]{:S(2)}, u32[]{:S(2)}) collective-permute-start(f32[2,8,3]{1,0,2:T(2,128)S(1)} %maximum_add_fusion.2), channel_id=1, source_target_pairs={{0,32},{32,64},{64,96},{96,128},{128,160},{160,192},{192,224},{224... | collective-permute-start | bytes 584 | tf_op jit(solution)/shard_map/while/body/eval_jaxpr/ppermute | solution.py:25
  74.7 7.6 %collective-permute-start = (f32[2,8,3]{1,0,2:T(2,128)S(1)}, f32[2,8,3]{1,0,2:T(2,128)S(1)}, u32[]{:S(2)}, u32[]{:S(2)}) collective-permute-start(f32[2,8,3]{1,0,2:T(2,128)S(1)} %maximum_add_fusion.2), channel_id=1, source_target_pairs={{0,32},{32,64},{64,96},{96,128},{128,160},{160,192},{192,224},{224... | collective-permute-start | bytes 584 | tf_op jit(solution)/shard_map/while/body/eval_jaxpr/ppermute | solution.py:25
  82.3 7.6 %collective-permute-start = (f32[2,8,3]{1,0,2:T(2,128)S(1)}, f32[2,8,3]{1,0,2:T(2,128)S(1)}, u32[]{:S(2)}, u32[]{:S(2)}) collective-permute-start(f32[2,8,3]{1,0,2:T(2,128)S(1)} %maximum_add_fusion.2), channel_id=1, source_target_pairs={{0,32},{32,64},{64,96},{96,128},{128,160},{160,192},{192,224},{224... | collective-permute-start | bytes 584 | tf_op jit(solution)/shard_map/while/body/eval_jaxpr/ppermute | solution.py:25
  89.9 7.6 %collective-permute-start = (f32[2,8,3]{1,0,2:T(2,128)S(1)}, f32[2,8,3]{1,0,2:T(2,128)S(1)}, u32[]{:S(2)}, u32[]{:S(2)}) collective-permute-start(f32[2,8,3]{1,0,2:T(2,128)S(1)} %maximum_add_fusion.2), channel_id=1, source_target_pairs={{0,32},{32,64},{64,96},{96,128},{128,160},{160,192},{192,224},{224... | collective-permute-start | bytes 584 | tf_op jit(solution)/shard_map/while/body/eval_jaxpr/ppermute | solution.py:25
  97.5 7.6 %collective-permute-start = (f32[2,8,3]{1,0,2:T(2,128)S(1)}, f32[2,8,3]{1,0,2:T(2,128)S(1)}, u32[]{:S(2)}, u32[]{:S(2)}) collective-permute-start(f32[2,8,3]{1,0,2:T(2,128)S(1)} %maximum_add_fusion.2), channel_id=1, source_target_pairs={{0,32},{32,64},{64,96},{96,128},{128,160},{160,192},{192,224},{224... | collective-permute-start | bytes 584 | tf_op jit(solution)/shard_map/while/body/eval_jaxpr/ppermute | solution.py:25
  105.1 7.6 %collective-permute-start = (f32[2,8,3]{1,0,2:T(2,128)S(1)}, f32[2,8,3]{1,0,2:T(2,128)S(1)}, u32[]{:S(2)}, u32[]{:S(2)}) collective-permute-start(f32[2,8,3]{1,0,2:T(2,128)S(1)} %maximum_add_fusion.2), channel_id=1, source_target_pairs={{0,32},{32,64},{64,96},{96,128},{128,160},{160,192},{192,224},{224... | collective-permute-start | bytes 584 | tf_op jit(solution)/shard_map/while/body/eval_jaxpr/ppermute | solution.py:25
  112.8 7.6 %collective-permute-start = (f32[2,8,3]{1,0,2:T(2,128)S(1)}, f32[2,8,3]{1,0,2:T(2,128)S(1)}, u32[]{:S(2)}, u32[]{:S(2)}) collective-permute-start(f32[2,8,3]{1,0,2:T(2,128)S(1)} %maximum_add_fusion.2), channel_id=1, source_target_pairs={{0,32},{32,64},{64,96},{96,128},{128,160},{160,192},{192,224},{224... | collective-permute-start | bytes 584 | tf_op jit(solution)/shard_map/while/body/eval_jaxpr/ppermute | solution.py:25
  120.4 7.6 %collective-permute-start = (f32[2,8,3]{1,0,2:T(2,128)S(1)}, f32[2,8,3]{1,0,2:T(2,128)S(1)}, u32[]{:S(2)}, u32[]{:S(2)}) collective-permute-start(f32[2,8,3]{1,0,2:T(2,128)S(1)} %maximum_add_fusion.2), channel_id=1, source_target_pairs={{0,32},{32,64},{64,96},{96,128},{128,160},{160,192},{192,224},{224... | collective-permute-start | bytes 584 | tf_op jit(solution)/shard_map/while/body/eval_jaxpr/ppermute | solution.py:25
  128.0 7.6 %collective-permute-start = (f32[2,8,3]{1,0,2:T(2,128)S(1)}, f32[2,8,3]{1,0,2:T(2,128)S(1)}, u32[]{:S(2)}, u32[]{:S(2)}) collective-permute-start(f32[2,8,3]{1,0,2:T(2,128)S(1)} %maximum_add_fusion.2), channel_id=1, source_target_pairs={{0,32},{32,64},{64,96},{96,128},{128,160},{160,192},{192,224},{224... | collective-permute-start | bytes 584 | tf_op jit(solution)/shard_map/while/body/eval_jaxpr/ppermute | solution.py:25
  135.6 7.6 %collective-permute-start = (f32[2,8,3]{1,0,2:T(2,128)S(1)}, f32[2,8,3]{1,0,2:T(2,128)S(1)}, u32[]{:S(2)}, u32[]{:S(2)}) collective-permute-start(f32[2,8,3]{1,0,2:T(2,128)S(1)} %maximum_add_fusion.2), channel_id=1, source_target_pairs={{0,32},{32,64},{64,96},{96,128},{128,160},{160,192},{192,224},{224... | collective-permute-start | bytes 584 | tf_op jit(solution)/shard_map/while/body/eval_jaxpr/ppermute | solution.py:25
  143.2 7.6 %collective-permute-start = (f32[2,8,3]{1,0,2:T(2,128)S(1)}, f32[2,8,3]{1,0,2:T(2,128)S(1)}, u32[]{:S(2)}, u32[]{:S(2)}) collective-permute-start(f32[2,8,3]{1,0,2:T(2,128)S(1)} %maximum_add_fusion.2), channel_id=1, source_target_pairs={{0,32},{32,64},{64,96},{96,128},{128,160},{160,192},{192,224},{224... | collective-permute-start | bytes 584 | tf_op jit(solution)/shard_map/while/body/eval_jaxpr/ppermute | solution.py:25
  150.9 7.6 %collective-permute-start = (f32[2,8,3]{1,0,2:T(2,128)S(1)}, f32[2,8,3]{1,0,2:T(2,128)S(1)}, u32[]{:S(2)}, u32[]{:S(2)}) collective-permute-start(f32[2,8,3]{1,0,2:T(2,128)S(1)} %maximum_add_fusion.2), channel_id=1, source_target_pairs={{0,32},{32,64},{64,96},{96,128},{128,160},{160,192},{192,224},{224... | collective-permute-start | bytes 584 | tf_op jit(solution)/shard_map/while/body/eval_jaxpr/ppermute | solution.py:25
  158.5 7.6 %collective-permute-start = (f32[2,8,3]{1,0,2:T(2,128)S(1)}, f32[2,8,3]{1,0,2:T(2,128)S(1)}, u32[]{:S(2)}, u32[]{:S(2)}) collective-permute-start(f32[2,8,3]{1,0,2:T(2,128)S(1)} %maximum_add_fusion.2), channel_id=1, source_target_pairs={{0,32},{32,64},{64,96},{96,128},{128,160},{160,192},{192,224},{224... | collective-permute-start | bytes 584 | tf_op jit(solution)/shard_map/while/body/eval_jaxpr/ppermute | solution.py:25
  361.5 0.6 copy-start.3
  367.9 0.9 copy-start
  368.8 0.7 copy-start.4
  371.5 5.6 %collective-permute-start.1 = (f32[6,384]{1,0:T(8,128)S(1)}, f32[6,384]{1,0:T(8,128)S(1)}, u32[]{:S(2)}, u32[]{:S(2)}) collective-permute-start(f32[6,384]{1,0:T(8,128)S(1)} %slice_select_fusion.1), channel_id=1, source_target_pairs={{32,0},{64,32},{96,64},{128,96},{160,128},{192,160},{224,192},{256... | collective-permute-start | bytes 27656 | tf_op jit(solution)/shard_map/ppermute | solution.py:25
  377.1 7.7 %collective-permute-start.2 = (f32[6,384]{1,0:T(8,128)S(1)}, f32[6,384]{1,0:T(8,128)S(1)}, u32[]{:S(2)}, u32[]{:S(2)}) collective-permute-start(f32[6,384]{1,0:T(8,128)S(1)} %get-tuple-element.114), channel_id=1, source_target_pairs={{0,32},{32,64},{64,96},{96,128},{128,160},{160,192},{192,224},{224... | collective-permute-start | bytes 27656 | tf_op jit(solution)/shard_map/ppermute | solution.py:25
  384.8 0.6 copy-start.5
